TPU v7x, 32 devices: a whole 2x2x4 slice. The times are simulated.
32 devices in a mesh: dp: 16 (over z, x, core), mp: 2 (over y).
Axes of the slice: x: 2, y: 2, z: 4, core: 2. Of those that a mesh axis runs over, the one named last changes fastest.
Arguments:
- features: bfloat16 [2048, 512], P('dp'), may hold values from -6 to 6
- w_in: bfloat16 [512, 512], P(None, 'mp'), may hold values from -0.25 to 0.25
- b_in: float32 [512], P('mp'), may hold values from -1 to 1
- w_out: bfloat16 [512, 128], P('mp'), may hold values from -0.25 to 0.25
- partner: int32 [2048], P('dp'), may hold values from 0 to 2047, as said below
- window: int32 [16], replicated, may hold values from 0 to 3
Outputs:
- row_loss: float32 [512], P('dp')
- grad_w_in: float32 [512, 512], P(None, 'mp')
- grad_b_in: float32 [512], P('mp')
- grad_w_out: float32 [512, 128], P('mp')
Inputs may be any that keep to these rules, and one draw needn't show every extreme that they name: partner pairs the rows: partner[partner[i]] = i and partner[i] != i for every row i.
All inputs are finite; a program needn't handle non-finite values.
Results may differ from a plain program's by a relative error of at most 0.0027.
Values may be sent and summed in bfloat16 or wider, within the bound.
A program may use at most 64 MiB of HBM per device.

v0:
```python
import math

import jax
import jax.numpy as jnp
from jax import lax
from jax.sharding import PartitionSpec as P

A_DEV = 32


INV_TEMP = 10.0
SHIFT = 10.0
EPS = 1e-06


def contract_rows(left, right):
    return lax.dot_general(
        left, right, (((0,), (0,)), ((), ())), preferred_element_type=jnp.float32
    )


def on_device(features, w_in, b_in, w_out, partner, window):
    rows = features.shape[0]
    parts = lax.axis_size("mp")
    part = lax.axis_index("mp")
    shards = lax.axis_size("dp")
    shard = lax.axis_index("dp")
    width = rows // parts
    anchor_rows = A_DEV
    anchor_all = anchor_rows * shards
    pre = jnp.dot(features, w_in, preferred_element_type=jnp.float32) + b_in
    hidden = jax.nn.silu(pre).astype(jnp.bfloat16)
    proj = lax.psum(jnp.dot(hidden, w_out, preferred_element_type=jnp.float32), "mp")
    norm = jnp.sqrt(jnp.sum(proj * proj, axis=1, keepdims=True) + EPS)
    emb = (proj / norm).astype(jnp.bfloat16)
    embed = emb.shape[1]
    own_cols = lax.dynamic_slice_in_dim(emb, part * width, width, 0)
    columns = lax.all_gather(own_cols, "dp", axis=0, tiled=True)
    col_total = columns.shape[0]
    shard_ids = jnp.arange(shards, dtype=jnp.int32)
    my_block = jnp.sum(jnp.where(shard_ids == shard, window, 0))
    my_start = my_block * anchor_rows
    anchors = lax.dynamic_slice_in_dim(emb, my_start, anchor_rows, 0)
    anchor_partner = lax.dynamic_slice_in_dim(partner, my_start, anchor_rows, 0)
    anchor_ids = shard * rows + my_start + jnp.arange(anchor_rows, dtype=jnp.int32)

    def column_ids(start, count):
        local = start + jnp.arange(count, dtype=jnp.int32)
        return local // width * rows + part * width + local % width

    blk = math.gcd(col_total, 2048)
    nblk = col_total // blk
    col_blocks = columns.reshape(nblk, blk, embed)
    starts = jnp.arange(nblk, dtype=jnp.int32) * blk

    def forward(carry, item):
        total, hit = carry
        block, start = item
        s = jnp.dot(anchors, block.T, preferred_element_type=jnp.float32) * INV_TEMP
        ids = column_ids(start, blk)
        ex = jnp.where(ids[None, :] == anchor_ids[:, None], 0.0, jnp.exp(s - SHIFT))
        hit = hit + jnp.sum(jnp.where(ids[None, :] == anchor_partner[:, None], s, 0.0), axis=1)
        return ((total + jnp.sum(ex, axis=1), hit), None)

    zero_rows = jnp.zeros((anchor_rows,), jnp.float32)
    (total, hit), _ = lax.scan(forward, (zero_rows, zero_rows), (col_blocks, starts))
    total, hit = lax.psum((total, hit), "mp")
    row_loss = jnp.log(total) + SHIFT - hit

    def row_weights(s, ids):
        prob = jnp.where(
            ids[None, :] == anchor_ids[:, None], 0.0, jnp.exp(s - SHIFT) / total[:, None]
        )
        onehot = (ids[None, :] == anchor_partner[:, None]).astype(jnp.float32)
        return (prob - onehot).astype(jnp.bfloat16)

    def backward(acc, item):
        block, start = item
        s = jnp.dot(anchors, block.T, preferred_element_type=jnp.float32) * INV_TEMP
        weights = row_weights(s, column_ids(start, blk))
        return (acc + jnp.dot(weights, block, preferred_element_type=jnp.float32), None)

    row_part, _ = lax.scan(
        backward, jnp.zeros((anchor_rows, embed), jnp.float32), (col_blocks, starts)
    )
    totals = lax.all_gather(total, "dp", axis=0, tiled=True)
    own_ids = shard * rows + part * width + jnp.arange(width, dtype=jnp.int32)
    own_partner = lax.dynamic_slice_in_dim(partner, part * width, width, 0)
    piece = lax.all_gather(anchors, "dp", axis=0, tiled=True)
    count = piece.shape[0]
    inner = math.gcd(count, 2048)
    sub_pieces = piece.reshape(count // inner, inner, embed)
    offsets = jnp.arange(count // inner, dtype=jnp.int32) * inner

    def one_block(inner_acc, item):
        block, offset = item
        block_totals = lax.dynamic_slice_in_dim(totals, offset, inner, 0)
        flat = offset + jnp.arange(inner, dtype=jnp.int32)
        owner = flat // anchor_rows
        owner_block = jnp.sum(
            jnp.where(owner[:, None] == shard_ids[None, :], window[None, :], 0), axis=1
        )
        ids = owner * rows + owner_block * anchor_rows + flat % anchor_rows
        s = jnp.dot(own_cols, block.T, preferred_element_type=jnp.float32) * INV_TEMP
        prob = jnp.where(
            ids[None, :] == own_ids[:, None], 0.0, jnp.exp(s - SHIFT) / block_totals[None, :]
        )
        onehot = (ids[None, :] == own_partner[:, None]).astype(jnp.float32)
        weights = (prob - onehot).astype(jnp.bfloat16)
        return (inner_acc + jnp.dot(weights, block, preferred_element_type=jnp.float32), None)

    result, _ = lax.scan(one_block, jnp.zeros((width, embed), jnp.float32), (sub_pieces, offsets))
    placed = lax.dynamic_update_slice_in_dim(
        jnp.zeros((rows, embed), jnp.float32), result, part * width, 0
    )
    row_placed = lax.dynamic_update_slice_in_dim(
        jnp.zeros((rows, embed), jnp.float32), row_part, my_start, 0
    )
    grad_emb = lax.psum(row_placed + placed, "mp") * (INV_TEMP / anchor_all)
    unit = proj / norm
    grad_proj = ((grad_emb - unit * jnp.sum(unit * grad_emb, axis=1, keepdims=True)) / norm).astype(
        jnp.bfloat16
    )
    grad_w_out = contract_rows(hidden, grad_proj)
    grad_hidden = lax.dot_general(
        grad_proj, w_out, (((1,), (1,)), ((), ())), preferred_element_type=jnp.float32
    )
    sig = jax.nn.sigmoid(pre)
    grad_pre = (grad_hidden * sig * (1.0 + pre * (1.0 - sig))).astype(jnp.bfloat16)
    grad_w_in = contract_rows(features, grad_pre)
    grad_b_in = jnp.sum(grad_pre.astype(jnp.float32), axis=0)
    grad_w_in, grad_b_in, grad_w_out = lax.psum((grad_w_in, grad_b_in, grad_w_out), "dp")
    return (row_loss, grad_w_in, grad_b_in, grad_w_out)


def solution(mesh):
    return jax.shard_map(
        on_device,
        mesh=mesh,
        in_specs=(P("dp", None), P(None, "mp"), P("mp"), P("mp", None), P("dp"), P()),
        out_specs=(P("dp"), P(None, "mp"), P("mp"), P("mp", None)),
        check_vma=False,
    )
```

profile of v0, /device:TPU:0, one launch (start us, length us, event | category | flops | bytes accessed | tf_op | source)
XLA Modules:
  0.0 234.8 jit_solution(11536599049466594532)
XLA Ops:
  7.2 0.9 copy-done
  8.1 1.1 multiply_convert_fusion
  9.3 0.8 fusion.57
  10.1 0.6 copy-done.7
  10.8 0.6 fusion.50
  12.1 0.6 copy-done.8
  13.0 0.6 copy-done.9
  13.7 0.6 dynamic-slice.3
  14.9 19.6 %all-reduce.7.cloned.1.call-done = f32[128,128]{1,0:T(8,128)} async-done(((f32[128,128]{1,0:T(8,128)}), f32[128,128]{1,0:T(8,128)}) %all-reduce.7.cloned.1.call-update) | async-done | bytes 65552 | tf_op jit(solution)/shard_map/psum | solution.py:33
  34.5 1.0 multiply_reduce_fusion.1
  35.7 21.7 %all_gather.10 = bf16[512,128]{1,0:T(8,128)(2,1)S(1)} all-gather(bf16[32,128]{1,0:T(8,128)(2,1)S(1)} %constant_dynamic-slice_fusion.1), channel_id=1, replica_groups=mesh['dp'=16,'mp'=2] {'dp'}, dimensions={0}, use_global_device_ids=true | all-gather | bytes 139264 | tf_op jit(solution)/shard_map/all_gather | solution.py:89
  57.4 18.1 %all_gather.9 = bf16[1024,128]{1,0:T(8,128)(2,1)S(1)} all-gather(bf16[64,128]{1,0:T(8,128)(2,1)S(1)} %constant_dynamic-slice_fusion), channel_id=1, replica_groups=mesh['dp'=16,'mp'=2] {'dp'}, dimensions={0}, use_global_device_ids=true | all-gather | bytes 278528 | tf_op jit(solution)/shard_map/all_gather | solution.py:38
  75.8 4.9 %all-reduce.2 = (f32[32]{0:T(128)S(1)}, f32[32]{0:T(128)S(1)}) all-reduce(f32[32]{0:T(128)S(1)} %get-tuple-element.70, f32[32]{0:T(128)S(1)} %get-tuple-element.69), channel_id=1, replica_groups=mesh['dp'=16,'mp'=2] {'mp'}, use_global_device_ids=true, to_apply=%region_6.7 | all-reduce | flops 64 | bytes 512 | tf_op jit(solution)/shard_map/psum | solution.py:67
  81.0 29.9 %all-reduce = f32[512]{0:T(512)S(1)} all-reduce(f32[512]{0:T(512)S(1)} %dynamic-update-slice.1), channel_id=1, replica_groups=mesh['dp'=16,'mp'=2] {'dp'}, use_global_device_ids=true, to_apply=%add | all-reduce | flops 512 | bytes 4096
  111.5 0.6 copy-done.3
  112.2 17.4 %all-reduce.9.cloned.1.call-done = f32[128,128]{1,0:T(8,128)} async-done(((f32[128,128]{1,0:T(8,128)}), f32[128,128]{1,0:T(8,128)}) %all-reduce.9.cloned.1.call-update) | async-done | bytes 65552 | tf_op jit(solution)/shard_map/psum | solution.py:119
  129.6 1.1 multiply_reduce_fusion
  130.8 0.9 fusion.58
  131.8 0.7 copy-done.5
  132.5 1.0 convolution_bitcast_fusion
  134.1 33.6 %psum.54 = f32[256]{0:T(256)} all-reduce(f32[256]{0:T(256)S(1)} %get-tuple-element.87), channel_id=1, replica_groups=mesh['dp'=16,'mp'=2] {'dp'}, use_global_device_ids=true, to_apply=%region_12.13 | all-reduce | flops 256 | bytes 2048 | tf_op jit(solution)/shard_map/psum | solution.py:132
  167.7 57.9 %all-reduce.11.cloned.1.call-done = (f32[512,256]{0,1:T(8,128)}, f32[256,128]{1,0:T(8,128)}) async-done(((f32[512,256]{0,1:T(8,128)}, f32[256,128]{1,0:T(8,128)}), (f32[512,256]{0,1:T(8,128)}, f32[256,128]{1,0:T(8,128)})) %all-reduce.11.cloned.1.call-update) | async-done | bytes 655376 | tf_op jit(solution)/shard_map/psum | solution.py:132
  225.5 2.1 copy.11
  227.6 0.7 copy.19
  (41 shorter events, 2.5 us)
Async XLA Ops:
  7.2 1.0 copy-start
  7.2 2.1 copy-start.6
  7.2 27.3 %all-reduce.7.cloned.1.call-start = ((), (), s32[]{:S(2)}) async-start(), calls=%async_computation | async-start | bytes 131072 | tf_op jit(solution)/shard_map/psum | solution.py:33
  10.1 119.5 %all-reduce.9.cloned.1.call-start = ((), (), s32[]{:S(2)}) async-start(), calls=%async_computation.1 | async-start | bytes 131072 | tf_op jit(solution)/shard_map/psum | solution.py:119
  10.1 0.7 copy-start.7
  12.1 0.7 copy-start.8
  13.0 0.7 copy-start.9
  34.5 1.0 copy-start.1
  111.4 0.6 copy-start.3
  112.1 113.4 %all-reduce.11.cloned.1.call-start = ((), (), s32[]{:S(2)}) async-start(), calls=%async_computation.2 | async-start | bytes 1310720 | tf_op jit(solution)/shard_map/psum | solution.py:132
  129.6 1.1 copy-start.2
  131.6 0.9 copy-start.5
  225.5 2.1 copy-start.4
Sparse Core Ops, SparseCore 0:
  10.8 23.6 all-reduce.6
  112.2 17.2 all-reduce.8
  133.7 91.7 all-reduce.10
where the time goes:
time: 235 us
  blocking collectives  108 us (46%)
  waiting for transfers between devices  94.9 us (40%)
  between operations  15.3 us (7%)
  local copies, waits for them, and re-layouts  7.86 us (3%)
  matrix products  4.84 us (2%)
  other arithmetic  3.56 us (2%)
    psum x1, waiting for transfers between devices, on_device(): lax.psum((grad_w_in, grad_b_in, grad_w_out), 'dp')  57.9 us
    psum x1, blocking collectives, on_device(): lax.psum((grad_w_in, grad_b_in, grad_w_out), 'dp')  33.6 us
    unnamed x1, blocking collectives  29.9 us
    all_gather x1, blocking collectives, on_device(): piece = lax.all_gather(anchors, 'dp', axis=0, tiled=True)  21.7 us
    psum x1, waiting for transfers between devices, on_device(): lax.psum(jnp.dot(hidden, w_out, preferred_element_type=jnp.float32), 'mp')  19.6 us
    all_gather x1, blocking collectives, on_device(): columns = lax.all_gather(own_cols, 'dp', axis=0, tiled=True)  18.1 us
    psum x1, waiting for transfers between devices, on_device(): grad_emb = lax.psum(row_placed + placed, 'mp') * (INV_TEMP / anchor_all)  17.4 us
    unnamed x25, local copies, waits for them, and re-layouts  7.68 us
  transfers between devices with their start and end apart: 3, of which 3 were waited for; matrix products, arithmetic and copies ran while one was open for 1% of the time, Pallas kernels for 0%

commit v1 on v0

v1 whole, which is shorter than its diff:
```python
import functools

import jax
import jax.numpy as jnp
from jax import lax
from jax.experimental import pallas as pl
from jax.experimental.pallas import tpu as pltpu
from jax.sharding import PartitionSpec as P

A_DEV = 32
INV_TEMP = 10.0
SHIFT = 10.0
EPS = 1e-06
LOG2E = 1.4426950408889634
MESH = pl.DeviceIdType.MESH
F32 = jnp.float32
BF16 = jnp.bfloat16


def dot(a, b, dims=((1,), (0,))):
    return lax.dot_general(a, b, (dims, ((), ())), preferred_element_type=F32)


def kernel(
    n, rows, tile, a_chunk,
    f_ref, wi_ref, bi_ref, wo_ref, part_ref, win_ref,
    loss_ref, gwi_ref, gbi_ref, gwo_ref,
    feat, part, wi2, bi2, wo2, hid, dsil, proj, emb, anch, ids, ex, gemb,
    f_send, f_recv, p_send, p_recv, w_send, w_recv, loc_sem,
):
    me = lax.axis_index("dp")
    other = 1 - lax.axis_index("mp")
    total = n * rows
    embed = wo_ref.shape[1]
    anchors = n * A_DEV

    barrier = pltpu.get_barrier_semaphore()
    pl.semaphore_signal(barrier, inc=1, device_id={"mp": other}, device_id_type=MESH)

    def greet(r, _):
        peer = lax.rem(me + r, n)
        pl.semaphore_signal(barrier, inc=1, device_id={"dp": peer}, device_id_type=MESH)
        return 0

    lax.fori_loop(1, n, greet, 0)
    own_f = pltpu.make_async_copy(f_ref, feat.at[pl.ds(me * rows, rows)], loc_sem.at[0])
    own_p = pltpu.make_async_copy(part_ref, part.at[me], loc_sem.at[1])
    own_f.start()
    own_p.start()
    pl.semaphore_wait(barrier, n)

    w_copies = [
        pltpu.make_async_remote_copy(
            src_ref=src, dst_ref=dst, send_sem=w_send.at[i], recv_sem=w_recv.at[i],
            device_id={"mp": other}, device_id_type=MESH,
        )
        for i, (src, dst) in enumerate(((wi_ref, wi2), (wo_ref, wo2), (bi_ref, bi2)))
    ]
    for copy in w_copies:
        copy.start()

    def f_copy(slot, peer):
        return pltpu.make_async_remote_copy(
            src_ref=f_ref, dst_ref=feat.at[pl.ds(slot * rows, rows)],
            send_sem=f_send.at[peer], recv_sem=f_recv.at[slot],
            device_id={"dp": peer}, device_id_type=MESH,
        )

    def p_copy(slot, peer):
        return pltpu.make_async_remote_copy(
            src_ref=part_ref, dst_ref=part.at[slot],
            send_sem=p_send.at[peer], recv_sem=p_recv.at[slot],
            device_id={"dp": peer}, device_id_type=MESH,
        )

    def send(r, _):
        peer = lax.rem(me + r, n)
        f_copy(me, peer).start()
        p_copy(me, peer).start()
        return 0

    lax.fori_loop(1, n, send, 0)
    own_f.wait()
    own_p.wait()
    for copy in w_copies:
        copy.wait()

    def receive(r, _):
        peer = lax.rem(me + r, n)
        f_copy(peer, peer).wait_recv()
        p_copy(peer, peer).wait_recv()
        f_copy(me, peer).wait_send()
        p_copy(me, peer).wait_send()
        return 0

    lax.fori_loop(1, n, receive, 0)

    def embed_rows(start, size):
        at = pl.ds(start, size)
        x = feat[at, :]
        pre = dot(x, wi_ref[...]) + bi_ref[...]
        sig = jax.nn.sigmoid(pre)
        h = (pre * sig).astype(BF16)
        hid[at, :] = h
        if dsil is not None:
            dsil[at, :] = sig * (1.0 + pre * (1.0 - sig))
        pre2 = dot(x, wi2[...]) + bi2[...]
        h2 = (pre2 * jax.nn.sigmoid(pre2)).astype(BF16)
        y = dot(h, wo_ref[...]) + dot(h2, wo2[...])
        proj[at, :] = y
        inv = lax.rsqrt(jnp.sum(y * y, axis=1, keepdims=True) + EPS)
        emb[at, :] = (y * inv).astype(BF16)
        gemb[at, :] = jnp.zeros((size, embed), F32)

    def embed_tile(t, _):
        embed_rows(pl.multiple_of(t * tile, tile), tile)
        return 0

    lax.fori_loop(0, total // tile, embed_tile, 0)

    def window_of(b):
        return jnp.full((A_DEV, embed), win_ref[b], jnp.int32)

    def gather(b, _):
        win = window_of(b)
        picked = jnp.zeros((A_DEV, embed), F32)
        for w in range(rows // A_DEV):
            at = pl.ds(pl.multiple_of(b * rows + w * A_DEV, A_DEV), A_DEV)
            picked = jnp.where(win == w, emb[at, :].astype(F32), picked)
        at = pl.ds(pl.multiple_of(b * A_DEV, A_DEV), A_DEV)
        anch[at, :] = picked.astype(BF16)
        first = b * rows + win * A_DEV
        ids[at, :] = first + lax.broadcasted_iota(jnp.int32, (A_DEV, embed), 0)
        return 0

    lax.fori_loop(0, n, gather, 0)

    blocks = tile // rows
    reps = tile // embed

    def ids_of(base, size):
        return jnp.tile(ids[pl.ds(base, size), :], (1, reps))

    def col_ids(start, size):
        return start + lax.broadcasted_iota(jnp.int32, (size, tile), 1)

    def part_row(t):
        pieces = [part[t * blocks + i] for i in range(blocks)]
        return jnp.concatenate(pieces, axis=1) if blocks > 1 else pieces[0]

    mine = pl.multiple_of(me * A_DEV, A_DEV)
    own_anch = anch[pl.ds(mine, A_DEV), :]
    own_ids = ids_of(mine, A_DEV)

    def own_tile(t, carry):
        tot, hit = carry
        start = pl.multiple_of(t * tile, tile)
        d = dot(own_anch, emb[pl.ds(start, tile), :], ((1,), (1,)))
        e = jnp.where(
            col_ids(start, A_DEV) == own_ids, 0.0,
            jnp.exp2(d * (INV_TEMP * LOG2E) - SHIFT * LOG2E),
        )
        tot = tot + jnp.sum(e, axis=1, keepdims=True)
        h = jnp.where(part_row(t) == own_ids, d, 0.0)
        return (tot, hit + jnp.sum(h, axis=1, keepdims=True))

    zero = jnp.zeros((A_DEV, 1), F32)
    tot, hit = lax.fori_loop(0, total // tile, own_tile, (zero, zero))
    loss = jnp.log(tot) + SHIFT - hit * INV_TEMP
    r_iota = lax.broadcasted_iota(jnp.int32, (A_DEV, A_DEV), 0)
    c_iota = lax.broadcasted_iota(jnp.int32, (A_DEV, A_DEV), 1)
    loss_ref[...] = jnp.sum(jnp.where(r_iota == c_iota, loss, 0.0), axis=0, keepdims=True)

    def loss_chunk(k, _):
        base = pl.multiple_of(k * a_chunk, a_chunk)
        anc = anch[pl.ds(base, a_chunk), :]
        a_ids = ids_of(base, a_chunk)

        def soft(t, tot):
            start = pl.multiple_of(t * tile, tile)
            d = dot(anc, emb[pl.ds(start, tile), :], ((1,), (1,)))
            e = jnp.where(
                col_ids(start, a_chunk) == a_ids, 0.0,
                jnp.exp2(d * (INV_TEMP * LOG2E) - SHIFT * LOG2E),
            )
            ex[:, pl.ds(start, tile)] = e
            return tot + jnp.sum(e, axis=1, keepdims=True)

        tot = lax.fori_loop(0, total // tile, soft, jnp.zeros((a_chunk, 1), F32))
        inv = 1.0 / tot

        def back(t, acc):
            start = pl.multiple_of(t * tile, tile)
            at = pl.ds(start, tile)
            onehot = jnp.where(part_row(t) == a_ids, 1.0, 0.0)
            w = (ex[:, at] * inv - onehot).astype(BF16)
            gemb[at, :] += dot(w, anc, ((0,), (0,)))
            return acc + dot(w, emb[at, :])

        row = lax.fori_loop(0, total // tile, back, jnp.zeros((a_chunk, embed), F32))
        for i in range(a_chunk // A_DEV):
            b = k * (a_chunk // A_DEV) + i
            piece = row[i * A_DEV:(i + 1) * A_DEV, :]
            win = window_of(b)
            for w in range(rows // A_DEV):
                at = pl.ds(pl.multiple_of(b * rows + w * A_DEV, A_DEV), A_DEV)
                gemb[at, :] += jnp.where(win == w, piece, 0.0)
        return 0

    lax.fori_loop(0, anchors // a_chunk, loss_chunk, 0)

    gwi_ref[...] = jnp.zeros_like(gwi_ref)
    gwo_ref[...] = jnp.zeros_like(gwo_ref)
    gbi_ref[...] = jnp.zeros_like(gbi_ref)

    def grads(t, _):
        at = pl.ds(pl.multiple_of(t * tile, tile), tile)
        y = proj[at, :]
        inv = lax.rsqrt(jnp.sum(y * y, axis=1, keepdims=True) + EPS)
        unit = y * inv
        g = gemb[at, :] * (INV_TEMP / anchors)
        gp = ((g - unit * jnp.sum(unit * g, axis=1, keepdims=True)) * inv).astype(BF16)
        x = feat[at, :]
        h = hid[at, :]
        gwo_ref[...] += dot(h, gp, ((0,), (0,)))
        if dsil is not None:
            slope = dsil[at, :]
        else:
            pre = dot(x, wi_ref[...]) + bi_ref[...]
            sig = jax.nn.sigmoid(pre)
            slope = sig * (1.0 + pre * (1.0 - sig))
        gpre = (dot(gp, wo_ref[...], ((1,), (1,))) * slope).astype(BF16)
        gwi_ref[...] += dot(x, gpre, ((0,), (0,)))
        gbi_ref[...] += jnp.sum(gpre.astype(F32), axis=0, keepdims=True)
        return 0

    lax.fori_loop(0, total // tile, grads, 0)


def no_slope(n, rows, tile, a_chunk, *refs):
    return kernel(n, rows, tile, a_chunk, *refs[:16], None, *refs[16:])


def on_device(features, w_in, b_in, w_out, partner, window):
    n = lax.axis_size("dp")
    rows, chan = features.shape
    half = w_in.shape[1]
    embed = w_out.shape[1]
    total = n * rows
    tile = 4 * rows if n % 4 == 0 else rows
    anchors = n * A_DEV
    a_chunk = 256
    while a_chunk > A_DEV and (a_chunk * total > 2 ** 19 or anchors % a_chunk):
        a_chunk //= 2
    keep = total * half <= 2 ** 20
    scratch = [
        pltpu.VMEM((total, chan), BF16),
        pltpu.VMEM((n, 1, rows), jnp.int32),
        pltpu.VMEM((chan, half), BF16),
        pltpu.VMEM((1, half), F32),
        pltpu.VMEM((half, embed), BF16),
        pltpu.VMEM((total, half), BF16),
    ]
    if keep:
        scratch.append(pltpu.VMEM((total, half), F32))
    scratch += [
        pltpu.VMEM((total, embed), F32),
        pltpu.VMEM((total, embed), BF16),
        pltpu.VMEM((anchors, embed), BF16),
        pltpu.VMEM((anchors, embed), jnp.int32),
        pltpu.VMEM((a_chunk, total), F32),
        pltpu.VMEM((total, embed), F32),
        pltpu.SemaphoreType.DMA((n,)),
        pltpu.SemaphoreType.DMA((n,)),
        pltpu.SemaphoreType.DMA((n,)),
        pltpu.SemaphoreType.DMA((n,)),
        pltpu.SemaphoreType.DMA((3,)),
        pltpu.SemaphoreType.DMA((3,)),
        pltpu.SemaphoreType.DMA((2,)),
    ]
    vmem = pl.BlockSpec(memory_space=pltpu.VMEM)
    loss, gwi, gbi, gwo = pl.pallas_call(
        functools.partial(kernel if keep else no_slope, n, rows, tile, a_chunk),
        out_shape=(
            jax.ShapeDtypeStruct((1, A_DEV), F32),
            jax.ShapeDtypeStruct((chan, half), F32),
            jax.ShapeDtypeStruct((1, half), F32),
            jax.ShapeDtypeStruct((half, embed), F32),
        ),
        in_specs=[vmem] * 5 + [pl.BlockSpec(memory_space=pltpu.SMEM)],
        out_specs=(vmem,) * 4,
        scratch_shapes=scratch,
        compiler_params=pltpu.CompilerParams(
            collective_id=0, has_side_effects=True, vmem_limit_bytes=67043328
        ),
    )(features, w_in, b_in.reshape(1, half), w_out, partner.reshape(1, rows), window)
    return (loss.reshape(A_DEV), gwi, gbi.reshape(half), gwo)


def solution(mesh):
    return jax.shard_map(
        on_device,
        mesh=mesh,
        in_specs=(P("dp", None), P(None, "mp"), P("mp"), P("mp", None), P("dp"), P()),
        out_specs=(P("dp"), P(None, "mp"), P("mp"), P("mp", None)),
        check_vma=False,
    )
```

time: 235 us -> 72 us (0.31)
  the two profiles are of different devices: /device:TPU:0 before, /device:TPU:11 now
where the time goes in v1:
time: 72 us; the launch traced here: 71.9 us
  Pallas kernels  67 us (93%)
  local copies, waits for them, and re-layouts  4.24 us (6%)
    pallas_call x1, Pallas kernels, on_device(): pl.pallas_call(functools.partial(kernel if keep else no_slope, n, rows, t...  67 us
    unnamed x10, local copies, waits for them, and re-layouts  4.24 us

profile of v1, /device:TPU:11, one launch (start us, length us, event | category | flops | bytes accessed | tf_op | source)
XLA Modules:
  0.0 71.9 jit_solution(11573748360115757328)
XLA Ops:
  0.6 67.0 %shard_map.93 = (f32[1,32]{1,0:T(1,128)}, f32[512,256]{1,0:T(8,128)}, f32[1,256]{1,0:T(1,128)}, f32[256,128]{1,0:T(8,128)}) custom-call(bf16[128,512]{1,0:T(8,128)(2,1)} %f_ref.1, bf16[512,256]{1,0:T(8,128)(2,1)} %wi_ref.1, f32[1,256]{1,0:T(1,128)} %bitcast.4, bf16[256,128]{1,0:T(8,128)(2,1)} %wo_ref.1, s32[1,128]{1,0:T(1,128)} %bitcast.6, s32[16]{0:T(128)} %win_ref.1), custom_call_target="tpu_custom_call" | custom-call | tf_op jit(solution)/shard_map/pallas_call | solution.py:282
  67.6 0.0 copy-start.2
  67.6 0.6 copy-done.2
  68.2 0.5 copy.14
  68.7 0.0 copy-start.1
  68.7 0.0 copy-start
  68.7 1.9 %copy.15 = f32[512,256]{1,0:T(8,128)} copy(f32[512,256]{1,0:T(8,128)} %get-tuple-element.17) | data formatting | bytes 1048576
  70.6 0.0 copy-done.1
  70.6 0.6 copy.16
  71.2 0.0 copy-done
  71.2 0.7 copy.17
Async XLA Ops:
  67.6 0.6 copy-start.2
  68.7 1.9 %copy-start.1 = (f32[1,256]{1,0:T(1,128)S(1)}, f32[1,256]{1,0:T(1,128)}, u32[]{:S(2)}) copy-start(f32[1,256]{1,0:T(1,128)} %get-tuple-element.10) | copy-start | bytes 3076
  68.7 2.5 %copy-start = (f32[256,128]{1,0:T(8,128)S(1)}, f32[256,128]{1,0:T(8,128)}, u32[]{:S(2)}) copy-start(f32[256,128]{1,0:T(8,128)} %get-tuple-element.19) | copy-start | bytes 393220

commit v2 on v1

--- a/solution.py
+++ b/solution.py
@@ -26,74 +26,184 @@
     f_ref, wi_ref, bi_ref, wo_ref, part_ref, win_ref,
     loss_ref, gwi_ref, gbi_ref, gwo_ref,
     feat, part, wi2, bi2, wo2, hid, dsil, proj, emb, anch, ids, ex, gemb,
-    f_send, f_recv, p_send, p_recv, w_send, w_recv, loc_sem,
+    send_sem, recv_sem, w_send, w_recv, loc_sem,
 ):
     me = lax.axis_index("dp")
     other = 1 - lax.axis_index("mp")
     total = n * rows
     embed = wo_ref.shape[1]
     anchors = n * A_DEV
+    chan, half = wi_ref.shape
+
+    depth = n // 4
+    z = me // 4
+    x_at = lax.rem(me // 2, 2)
+    core = lax.rem(me, 2)
+    links = (me - 4, me + 4, me + 2 - 4 * x_at, me + 1 - 2 * core)
+    LEFT, RIGHT, ACROSS, SIBLING = range(4)
+    has_left = z > 0
+    has_right = z < depth - 1
 
     barrier = pltpu.get_barrier_semaphore()
-    pl.semaphore_signal(barrier, inc=1, device_id={"mp": other}, device_id_type=MESH)
-
-    def greet(r, _):
-        peer = lax.rem(me + r, n)
-        pl.semaphore_signal(barrier, inc=1, device_id={"dp": peer}, device_id_type=MESH)
-        return 0
-
-    lax.fori_loop(1, n, greet, 0)
+
+    def greet(where):
+        pl.semaphore_signal(barrier, inc=1, device_id=where, device_id_type=MESH)
+
+    greet({"mp": other})
+    greet({"dp": links[ACROSS]})
+    greet({"dp": links[SIBLING]})
+
+    @pl.when(has_left)
+    def _():
+        greet({"dp": links[LEFT]})
+
+    @pl.when(has_right)
+    def _():
+        greet({"dp": links[RIGHT]})
+
     own_f = pltpu.make_async_copy(f_ref, feat.at[pl.ds(me * rows, rows)], loc_sem.at[0])
     own_p = pltpu.make_async_copy(part_ref, part.at[me], loc_sem.at[1])
     own_f.start()
     own_p.start()
-    pl.semaphore_wait(barrier, n)
-
-    w_copies = [
-        pltpu.make_async_remote_copy(
-            src_ref=src, dst_ref=dst, send_sem=w_send.at[i], recv_sem=w_recv.at[i],
-            device_id={"mp": other}, device_id_type=MESH,
+    pl.semaphore_wait(
+        barrier, 3 + jnp.where(has_left, 1, 0) + jnp.where(has_right, 1, 0)
+    )
+
+    cut = rows // 2
+
+    def item(kind, slot, dest, own=False):
+        if kind == 2:
+            dst = part.at[slot]
+            src = part_ref if own else dst
+        else:
+            dst = feat.at[pl.ds(slot * rows + kind * cut, cut)]
+            src = f_ref.at[pl.ds(kind * cut, cut)] if own else dst
+        return pltpu.make_async_remote_copy(
+            src_ref=src, dst_ref=dst,
+            send_sem=send_sem.at[(kind * 4 + dest) * n + slot],
+            recv_sem=recv_sem.at[kind * n + slot],
+            device_id={"dp": links[dest]}, device_id_type=MESH,
         )
-        for i, (src, dst) in enumerate(((wi_ref, wi2), (wo_ref, wo2), (bi_ref, bi2)))
-    ]
-    for copy in w_copies:
+
+    def got(kind, slot):
+        item(kind, slot, SIBLING).wait_recv()
+
+    wi_cut, wo_cut = chan // 2, half // 2
+
+    def weights(base, device, relay, c):
+        wi_at = pl.ds(c * wi_cut, wi_cut)
+        wo_at = pl.ds(c * wo_cut, wo_cut)
+        pairs = [
+            ((wi2 if relay else wi_ref).at[wi_at], wi2.at[wi_at]),
+            ((wo2 if relay else wo_ref).at[wo_at], wo2.at[wo_at]),
+        ]
+        if not relay:
+            pairs.append((bi_ref, bi2))
+        return [
+            pltpu.make_async_remote_copy(
+                src_ref=src, dst_ref=dst, send_sem=w_send.at[base + i],
+                recv_sem=w_recv.at[base + i], device_id=device, device_id_type=MESH,
+            )
+            for i, (src, dst) in enumerate(pairs)
+        ]
+
+    w_out_copies = weights(0, {"mp": other}, False, core)
+    w_relays = weights(3, {"dp": links[SIBLING]}, True, core)
+    w_from_sib = weights(3, {"dp": links[SIBLING]}, True, 1 - core)
+
+    def to(kind, slot, dest, start, own=False):
+        copy = item(kind, slot, dest, own)
+        if start:
+            copy.start()
+        else:
+            copy.wait_send()
+
+    def sides(kind, slot, start, own=False):
+        @pl.when(has_left)
+        def _():
+            to(kind, slot, LEFT, start, own)
+
+        @pl.when(has_right)
+        def _():
+            to(kind, slot, RIGHT, start, own)
+
+    def own_sends(start):
+        for kind in (0, 1, 2):
+            sides(kind, me, start, True)
+            to(kind, me, ACROSS, start, True)
+        for kind in (0, 1, 2):
+            to(kind, me, SIBLING, start, True)
+
+    def first_step(start):
+        slot = links[ACROSS]
+        if start:
+            got(1, slot)
+        sides(1, slot, start)
+        to(1, slot, SIBLING, start)
+        for kind in (0, 2):
+            if start:
+                got(kind, slot)
+            to(kind, slot, SIBLING, start)
+
+    def from_side(slot, dest, more, start):
+        twin = slot + links[ACROSS] - me
+        for kind, source in ((0, slot), (1, slot), (1, twin), (2, slot)):
+            if start:
+                got(kind, source)
+
+            @pl.when(more)
+            def _():
+                to(kind, source, dest, start)
+
+            if source is slot and kind != 1:
+                to(kind, source, ACROSS, start)
+            to(kind, source, SIBLING, start)
+
+    def from_across(slot, start):
+        twin = slot + links[ACROSS] - me
+        for kind in (0, 2):
+            if start:
+                got(kind, twin)
+            to(kind, twin, SIBLING, start)
+
+    def later_step(t, start):
+        @pl.when(z - t >= 0)
+        def _():
+            from_side(me - 4 * t, RIGHT, has_right, start)
+
+        @pl.when(z + t < depth)
+        def _():
+            from_side(me + 4 * t, LEFT, has_left, start)
+
+        @pl.when(z - t >= 0)
+        def _():
+            from_across(me - 4 * t, start)
+
+        @pl.when(z + t < depth)
+        def _():
+            from_across(me + 4 * t, start)
+
+    own_sends(True)
+    for copy in w_out_copies:
         copy.start()
-
-    def f_copy(slot, peer):
-        return pltpu.make_async_remote_copy(
-            src_ref=f_ref, dst_ref=feat.at[pl.ds(slot * rows, rows)],
-            send_sem=f_send.at[peer], recv_sem=f_recv.at[slot],
-            device_id={"dp": peer}, device_id_type=MESH,
-        )
-
-    def p_copy(slot, peer):
-        return pltpu.make_async_remote_copy(
-            src_ref=part_ref, dst_ref=part.at[slot],
-            send_sem=p_send.at[peer], recv_sem=p_recv.at[slot],
-            device_id={"dp": peer}, device_id_type=MESH,
-        )
-
-    def send(r, _):
-        peer = lax.rem(me + r, n)
-        f_copy(me, peer).start()
-        p_copy(me, peer).start()
-        return 0
-
-    lax.fori_loop(1, n, send, 0)
+    first_step(True)
+    for copy in w_out_copies:
+        copy.wait_recv()
+    for copy in w_relays:
+        copy.start()
+    lax.fori_loop(1, depth, lambda t, _: (later_step(t, True), 0)[1], 0)
     own_f.wait()
     own_p.wait()
-    for copy in w_copies:
-        copy.wait()
-
-    def receive(r, _):
-        peer = lax.rem(me + r, n)
-        f_copy(peer, peer).wait_recv()
-        p_copy(peer, peer).wait_recv()
-        f_copy(me, peer).wait_send()
-        p_copy(me, peer).wait_send()
+    for copy in w_from_sib:
+        copy.wait_recv()
+
+    def sibling_chip(q, _):
+        slot = q * 2 + 1 - core
+        for kind in (0, 1, 2):
+            got(kind, slot)
         return 0
 
-    lax.fori_loop(1, n, receive, 0)
+    lax.fori_loop(0, n // 2, sibling_chip, 0)
 
     def embed_rows(start, size):
         at = pl.ds(start, size)
@@ -235,6 +345,12 @@
         return 0
 
     lax.fori_loop(0, total // tile, grads, 0)
+
+    own_sends(False)
+    first_step(False)
+    lax.fori_loop(1, depth, lambda t, _: (later_step(t, False), 0)[1], 0)
+    for copy in w_out_copies + w_relays:
+        copy.wait_send()
 
 
 def no_slope(n, rows, tile, a_chunk, *refs):
@@ -270,12 +386,10 @@
         pltpu.VMEM((anchors, embed), jnp.int32),
         pltpu.VMEM((a_chunk, total), F32),
         pltpu.VMEM((total, embed), F32),
-        pltpu.SemaphoreType.DMA((n,)),
-        pltpu.SemaphoreType.DMA((n,)),
-        pltpu.SemaphoreType.DMA((n,)),
-        pltpu.SemaphoreType.DMA((n,)),
-        pltpu.SemaphoreType.DMA((3,)),
-        pltpu.SemaphoreType.DMA((3,)),
+        pltpu.SemaphoreType.DMA((12 * n,)),
+        pltpu.SemaphoreType.DMA((3 * n,)),
+        pltpu.SemaphoreType.DMA((5,)),
+        pltpu.SemaphoreType.DMA((5,)),
         pltpu.SemaphoreType.DMA((2,)),
     ]
     vmem = pl.BlockSpec(memory_space=pltpu.VMEM)

time: 72 us -> 46.7 us (0.65)
  the two profiles are of different devices: /device:TPU:11 before, /device:TPU:0 now
where the time goes in v2:
time: 46.7 us; the launch traced here: 45.9 us
  Pallas kernels  41 us (88%)
  local copies, waits for them, and re-layouts  4.24 us (9%)
  between operations  0.65 us (1%)
    pallas_call x1, Pallas kernels, on_device(): pl.pallas_call(functools.partial(kernel if keep else no_slope, n, rows, t...  41 us
    unnamed x10, local copies, waits for them, and re-layouts  4.24 us

profile of v2, /device:TPU:0, one launch (start us, length us, event | category | flops | bytes accessed | tf_op | source)
XLA Modules:
  0.0 45.9 jit_solution(17252199330595996856)
XLA Ops:
  0.6 41.0 %shard_map.93 = (f32[1,32]{1,0:T(1,128)}, f32[512,256]{1,0:T(8,128)}, f32[1,256]{1,0:T(1,128)}, f32[256,128]{1,0:T(8,128)}) custom-call(bf16[128,512]{1,0:T(8,128)(2,1)} %f_ref.1, bf16[512,256]{1,0:T(8,128)(2,1)} %wi_ref.1, f32[1,256]{1,0:T(1,128)} %bitcast.4, bf16[256,128]{1,0:T(8,128)(2,1)} %wo_ref.1, s32[1,128]{1,0:T(1,128)} %bitcast.6, s32[16]{0:T(128)} %win_ref.1), custom_call_target="tpu_custom_call" | custom-call | tf_op jit(solution)/shard_map/pallas_call | solution.py:396
  41.7 0.0 copy-start.2
  41.7 0.6 %copy-done.2 = f32[1,32]{1,0:T(1,128)S(1)} copy-done((f32[1,32]{1,0:T(1,128)S(1)}, f32[1,32]{1,0:T(1,128)}, u32[]{:S(2)}) %copy-start.2) | copy-done | bytes 152
  42.3 0.5 %copy.14 = f32[32]{0:T(128)} copy(f32[32]{0:T(128)S(1)} %bitcast.7) | data formatting | bytes 256
  42.8 0.0 copy-start.1
  42.8 0.0 copy-start
  42.8 1.9 %copy.15 = f32[512,256]{1,0:T(8,128)} copy(f32[512,256]{1,0:T(8,128)} %get-tuple-element.17) | data formatting | bytes 1048576
  44.7 0.0 copy-done.1
  44.7 0.6 %copy.16 = f32[256]{0:T(256)} copy(f32[256]{0:T(256)S(1)} %bitcast.5) | data formatting | bytes 2048
  45.3 0.0 copy-done
  45.3 0.7 %copy.17 = f32[256,128]{1,0:T(8,128)} copy(f32[256,128]{1,0:T(8,128)S(1)} %copy-done) | data formatting | bytes 262144
Async XLA Ops:
  41.7 0.6 %copy-start.2 = (f32[1,32]{1,0:T(1,128)S(1)}, f32[1,32]{1,0:T(1,128)}, u32[]{:S(2)}) copy-start(f32[1,32]{1,0:T(1,128)} %get-tuple-element.8) | copy-start | bytes 388
  42.8 1.9 %copy-start.1 = (f32[1,256]{1,0:T(1,128)S(1)}, f32[1,256]{1,0:T(1,128)}, u32[]{:S(2)}) copy-start(f32[1,256]{1,0:T(1,128)} %get-tuple-element.10) | copy-start | bytes 3076
  42.8 2.5 %copy-start = (f32[256,128]{1,0:T(8,128)S(1)}, f32[256,128]{1,0:T(8,128)}, u32[]{:S(2)}) copy-start(f32[256,128]{1,0:T(8,128)} %get-tuple-element.19) | copy-start | bytes 393220

commit v3 on v2

--- a/solution.py
+++ b/solution.py
@@ -8,6 +8,7 @@
 from jax.sharding import PartitionSpec as P
 
 A_DEV = 32
+PAD = 16
 INV_TEMP = 10.0
 SHIFT = 10.0
 EPS = 1e-06
@@ -61,32 +62,30 @@
     def _():
         greet({"dp": links[RIGHT]})
 
-    own_f = pltpu.make_async_copy(f_ref, feat.at[pl.ds(me * rows, rows)], loc_sem.at[0])
-    own_p = pltpu.make_async_copy(part_ref, part.at[me], loc_sem.at[1])
+    slot_rows = rows + PAD
+    own_f = pltpu.make_async_copy(
+        f_ref, feat.at[pl.ds(me * slot_rows, rows)], loc_sem.at[0]
+    )
     own_f.start()
-    own_p.start()
+    ints = part_ref[...]
+    pair = jnp.concatenate([ints // rows, lax.rem(ints, rows)], axis=1).astype(F32)
+    feat[pl.ds(pl.multiple_of(me * slot_rows + rows, PAD), PAD), 0:2 * rows] = (
+        jnp.broadcast_to(pair, (PAD, 2 * rows)).astype(BF16)
+    )
     pl.semaphore_wait(
         barrier, 3 + jnp.where(has_left, 1, 0) + jnp.where(has_right, 1, 0)
     )
 
-    cut = rows // 2
-
-    def item(kind, slot, dest, own=False):
-        if kind == 2:
-            dst = part.at[slot]
-            src = part_ref if own else dst
-        else:
-            dst = feat.at[pl.ds(slot * rows + kind * cut, cut)]
-            src = f_ref.at[pl.ds(kind * cut, cut)] if own else dst
+    def item(slot, dest):
+        ref = feat.at[pl.ds(slot * slot_rows, slot_rows)]
         return pltpu.make_async_remote_copy(
-            src_ref=src, dst_ref=dst,
-            send_sem=send_sem.at[(kind * 4 + dest) * n + slot],
-            recv_sem=recv_sem.at[kind * n + slot],
+            src_ref=ref, dst_ref=ref,
+            send_sem=send_sem.at[dest * n + slot], recv_sem=recv_sem.at[slot],
             device_id={"dp": links[dest]}, device_id_type=MESH,
         )
 
-    def got(kind, slot):
-        item(kind, slot, SIBLING).wait_recv()
+    def got(slot):
+        item(slot, SIBLING).wait_recv()
 
     wi_cut, wo_cut = chan // 2, half // 2
 
@@ -111,103 +110,86 @@
     w_relays = weights(3, {"dp": links[SIBLING]}, True, core)
     w_from_sib = weights(3, {"dp": links[SIBLING]}, True, 1 - core)
 
-    def to(kind, slot, dest, start, own=False):
-        copy = item(kind, slot, dest, own)
+    def to(slot, dest, start):
         if start:
-            copy.start()
+            item(slot, dest).start()
         else:
-            copy.wait_send()
-
-    def sides(kind, slot, start, own=False):
+            item(slot, dest).wait_send()
+
+    def sides(slot, start):
         @pl.when(has_left)
         def _():
-            to(kind, slot, LEFT, start, own)
+            to(slot, LEFT, start)
 
         @pl.when(has_right)
         def _():
-            to(kind, slot, RIGHT, start, own)
+            to(slot, RIGHT, start)
+
+    along = core == 0
+    twin_off = links[ACROSS] - me
 
     def own_sends(start):
-        for kind in (0, 1, 2):
-            sides(kind, me, start, True)
-            to(kind, me, ACROSS, start, True)
-        for kind in (0, 1, 2):
-            to(kind, me, SIBLING, start, True)
+        to(me, ACROSS, start)
+        sides(me, start)
+        to(me, SIBLING, start)
 
     def first_step(start):
-        slot = links[ACROSS]
+        slot = me + twin_off
         if start:
-            got(1, slot)
-        sides(1, slot, start)
-        to(1, slot, SIBLING, start)
-        for kind in (0, 2):
-            if start:
-                got(kind, slot)
-            to(kind, slot, SIBLING, start)
+            got(slot)
+
+        @pl.when(core == 1)
+        def _():
+            sides(slot, start)
+
+        to(slot, SIBLING, start)
 
     def from_side(slot, dest, more, start):
-        twin = slot + links[ACROSS] - me
-        for kind, source in ((0, slot), (1, slot), (1, twin), (2, slot)):
-            if start:
-                got(kind, source)
-
-            @pl.when(more)
+        if start:
+            got(slot)
+
+        @pl.when(more)
+        def _():
+            to(slot, dest, start)
+
+        @pl.when(along)
+        def _():
+            to(slot, ACROSS, start)
+
+        to(slot, SIBLING, start)
+
+    def twin_of(slot, dest, more, start):
+        twin = slot + twin_off
+        if start:
+            got(twin)
+
+        @pl.when(more & (core == 1))
+        def _():
+            to(twin, dest, start)
+
+        to(twin, SIBLING, start)
+
+    def later_step(t, start):
+        for each in (from_side, twin_of):
+            @pl.when(z - t >= 0)
             def _():
-                to(kind, source, dest, start)
-
-            if source is slot and kind != 1:
-                to(kind, source, ACROSS, start)
-            to(kind, source, SIBLING, start)
-
-    def from_across(slot, start):
-        twin = slot + links[ACROSS] - me
-        for kind in (0, 2):
-            if start:
-                got(kind, twin)
-            to(kind, twin, SIBLING, start)
-
-    def later_step(t, start):
-        @pl.when(z - t >= 0)
-        def _():
-            from_side(me - 4 * t, RIGHT, has_right, start)
-
-        @pl.when(z + t < depth)
-        def _():
-            from_side(me + 4 * t, LEFT, has_left, start)
-
-        @pl.when(z - t >= 0)
-        def _():
-            from_across(me - 4 * t, start)
-
-        @pl.when(z + t < depth)
-        def _():
-            from_across(me + 4 * t, start)
-
-    own_sends(True)
-    for copy in w_out_copies:
-        copy.start()
-    first_step(True)
-    for copy in w_out_copies:
-        copy.wait_recv()
-    for copy in w_relays:
-        copy.start()
-    lax.fori_loop(1, depth, lambda t, _: (later_step(t, True), 0)[1], 0)
-    own_f.wait()
-    own_p.wait()
-    for copy in w_from_sib:
-        copy.wait_recv()
-
-    def sibling_chip(q, _):
-        slot = q * 2 + 1 - core
-        for kind in (0, 1, 2):
-            got(kind, slot)
-        return 0
-
-    lax.fori_loop(0, n // 2, sibling_chip, 0)
-
-    def embed_rows(start, size):
-        at = pl.ds(start, size)
-        x = feat[at, :]
+                each(me - 4 * t, RIGHT, has_right, start)
+
+            @pl.when(z + t < depth)
+            def _():
+                each(me + 4 * t, LEFT, has_left, start)
+
+    def feat_rows(first, count):
+        pieces = [
+            feat[pl.ds(pl.multiple_of((first + i) * slot_rows, PAD), rows), :]
+            for i in range(count)
+        ]
+        return jnp.concatenate(pieces, axis=0)
+
+    def embed_chip(chip):
+        first = chip * 2
+        at = pl.ds(pl.multiple_of(first * rows, 2 * rows), 2 * rows)
+        x = feat_rows(first, 2)
         pre = dot(x, wi_ref[...]) + bi_ref[...]
         sig = jax.nn.sigmoid(pre)
         h = (pre * sig).astype(BF16)
@@ -220,13 +202,45 @@
         proj[at, :] = y
         inv = lax.rsqrt(jnp.sum(y * y, axis=1, keepdims=True) + EPS)
         emb[at, :] = (y * inv).astype(BF16)
-        gemb[at, :] = jnp.zeros((size, embed), F32)
-
-    def embed_tile(t, _):
-        embed_rows(pl.multiple_of(t * tile, tile), tile)
+        gemb[at, :] = jnp.zeros((2 * rows, embed), F32)
+
+    own_f.wait()
+    own_sends(True)
+    for copy in w_out_copies:
+        copy.start()
+    first_step(True)
+    for copy in w_out_copies:
+        copy.wait_recv()
+    for copy in w_relays:
+        copy.start()
+
+    def gather_step(t, _):
+        @pl.when(t < depth)
+        def _():
+            later_step(t, True)
+
+        @pl.when(t == 1)
+        def _():
+            for copy in w_from_sib:
+                copy.wait_recv()
+
+        def one(j, _):
+            step = t - 1
+            z_from = jnp.where(j < 2, z - step, z + step)
+            chip = z_from * 2 + lax.rem(j, 2)
+            ok = (z_from >= 0) & (z_from < depth) & ((j < 2) | (step > 0))
+
+            @pl.when(ok)
+            def _():
+                got(chip * 2 + 1 - core)
+                embed_chip(chip)
+
+            return 0
+
+        lax.fori_loop(0, 4, one, 0)
         return 0
 
-    lax.fori_loop(0, total // tile, embed_tile, 0)
+    lax.fori_loop(1, depth + 1, gather_step, 0)
 
     def window_of(b):
         return jnp.full((A_DEV, embed), win_ref[b], jnp.int32)
@@ -254,6 +268,14 @@
     def col_ids(start, size):
         return start + lax.broadcasted_iota(jnp.int32, (size, tile), 1)
 
+    def unpack(t, _):
+        r = feat[pl.ds(pl.multiple_of(t * slot_rows + rows, PAD), PAD), 0:2 * rows]
+        v = r.astype(F32).astype(jnp.int32)
+        part[t] = v[0:1, :rows] * rows + v[0:1, rows:]
+        return 0
+
+    lax.fori_loop(0, n, unpack, 0)
+
     def part_row(t):
         pieces = [part[t * blocks + i] for i in range(blocks)]
         return jnp.concatenate(pieces, axis=1) if blocks > 1 else pieces[0]
@@ -330,7 +352,7 @@
         unit = y * inv
         g = gemb[at, :] * (INV_TEMP / anchors)
         gp = ((g - unit * jnp.sum(unit * g, axis=1, keepdims=True)) * inv).astype(BF16)
-        x = feat[at, :]
+        x = feat_rows(t * blocks, blocks)
         h = hid[at, :]
         gwo_ref[...] += dot(h, gp, ((0,), (0,)))
         if dsil is not None:
@@ -370,7 +392,7 @@
         a_chunk //= 2
     keep = total * half <= 2 ** 20
     scratch = [
-        pltpu.VMEM((total, chan), BF16),
+        pltpu.VMEM((n * (rows + PAD), chan), BF16),
         pltpu.VMEM((n, 1, rows), jnp.int32),
         pltpu.VMEM((chan, half), BF16),
         pltpu.VMEM((1, half), F32),
@@ -386,11 +408,11 @@
         pltpu.VMEM((anchors, embed), jnp.int32),
         pltpu.VMEM((a_chunk, total), F32),
         pltpu.VMEM((total, embed), F32),
-        pltpu.SemaphoreType.DMA((12 * n,)),
-        pltpu.SemaphoreType.DMA((3 * n,)),
+        pltpu.SemaphoreType.DMA((4 * n,)),
+        pltpu.SemaphoreType.DMA((n,)),
         pltpu.SemaphoreType.DMA((5,)),
         pltpu.SemaphoreType.DMA((5,)),
-        pltpu.SemaphoreType.DMA((2,)),
+        pltpu.SemaphoreType.DMA((1,)),
     ]
     vmem = pl.BlockSpec(memory_space=pltpu.VMEM)
     loss, gwi, gbi, gwo = pl.pallas_call(

time: 46.7 us -> 45.6 us (0.976); the launches traced: 45.9 us -> 45.4 us
  Pallas kernels: 41 us -> 40.5 us
    pallas_call x1, Pallas kernels: 41 us -> 40.5 us  [on_device(): pl.pallas_call(functools.partial(kernel if keep else no_slope, n, rows, t...]
where the time goes in v3:
time: 45.6 us; the launch traced here: 45.4 us
  Pallas kernels  40.5 us (89%)
  local copies, waits for them, and re-layouts  4.24 us (9%)
  between operations  0.65 us (1%)
    pallas_call x1, Pallas kernels, on_device(): pl.pallas_call(functools.partial(kernel if keep else no_slope, n, rows, t...  40.5 us
    unnamed x10, local copies, waits for them, and re-layouts  4.24 us

profile of v3, /device:TPU:0, one launch (start us, length us, event | category | flops | bytes accessed | tf_op | source)
XLA Modules:
  0.0 45.4 jit_solution(16029366236268163489)
XLA Ops:
  0.6 40.5 %shard_map.93 = (f32[1,32]{1,0:T(1,128)}, f32[512,256]{1,0:T(8,128)}, f32[1,256]{1,0:T(1,128)}, f32[256,128]{1,0:T(8,128)}) custom-call(bf16[128,512]{1,0:T(8,128)(2,1)} %f_ref.1, bf16[512,256]{1,0:T(8,128)(2,1)} %wi_ref.1, f32[1,256]{1,0:T(1,128)} %bitcast.4, bf16[256,128]{1,0:T(8,128)(2,1)} %wo_ref.1, s32[1,128]{1,0:T(1,128)} %bitcast.6, s32[16]{0:T(128)} %win_ref.1), custom_call_target="tpu_custom_call" | custom-call | tf_op jit(solution)/shard_map/pallas_call | solution.py:418
  41.1 0.0 copy-start.2
  41.1 0.6 %copy-done.2 = f32[1,32]{1,0:T(1,128)S(1)} copy-done((f32[1,32]{1,0:T(1,128)S(1)}, f32[1,32]{1,0:T(1,128)}, u32[]{:S(2)}) %copy-start.2) | copy-done | bytes 152
  41.7 0.5 %copy.14 = f32[32]{0:T(128)} copy(f32[32]{0:T(128)S(1)} %bitcast.7) | data formatting | bytes 256
  42.3 0.0 copy-start.1
  42.3 0.0 copy-start
  42.3 1.9 %copy.15 = f32[512,256]{1,0:T(8,128)} copy(f32[512,256]{1,0:T(8,128)} %get-tuple-element.17) | data formatting | bytes 1048576
  44.2 0.0 copy-done.1
  44.2 0.6 %copy.16 = f32[256]{0:T(256)} copy(f32[256]{0:T(256)S(1)} %bitcast.5) | data formatting | bytes 2048
  44.7 0.0 copy-done
  44.7 0.7 %copy.17 = f32[256,128]{1,0:T(8,128)} copy(f32[256,128]{1,0:T(8,128)S(1)} %copy-done) | data formatting | bytes 262144
Async XLA Ops:
  41.1 0.6 %copy-start.2 = (f32[1,32]{1,0:T(1,128)S(1)}, f32[1,32]{1,0:T(1,128)}, u32[]{:S(2)}) copy-start(f32[1,32]{1,0:T(1,128)} %get-tuple-element.8) | copy-start | bytes 388
  42.3 1.9 %copy-start.1 = (f32[1,256]{1,0:T(1,128)S(1)}, f32[1,256]{1,0:T(1,128)}, u32[]{:S(2)}) copy-start(f32[1,256]{1,0:T(1,128)} %get-tuple-element.10) | copy-start | bytes 3076
  42.3 2.5 %copy-start = (f32[256,128]{1,0:T(8,128)S(1)}, f32[256,128]{1,0:T(8,128)}, u32[]{:S(2)}) copy-start(f32[256,128]{1,0:T(8,128)} %get-tuple-element.19) | copy-start | bytes 393220

commit v4 on v3

--- a/solution.py
+++ b/solution.py
@@ -377,6 +377,30 @@
 
 def no_slope(n, rows, tile, a_chunk, *refs):
     return kernel(n, rows, tile, a_chunk, *refs[:16], None, *refs[16:])
+
+
+def hand_out(*arrays):
+    count = len(arrays)
+
+    def copy_all(*refs):
+        sems = refs[-1]
+        copies = [
+            pltpu.make_async_copy(refs[i], refs[count + i], sems.at[i])
+            for i in range(count)
+        ]
+        for copy in copies:
+            copy.start()
+        for copy in copies:
+            copy.wait()
+
+    return pl.pallas_call(
+        copy_all,
+        out_shape=[jax.ShapeDtypeStruct(a.shape, a.dtype) for a in arrays],
+        in_specs=[pl.BlockSpec(memory_space=pltpu.VMEM)] * count,
+        out_specs=[pl.BlockSpec(memory_space=pl.ANY)] * count,
+        scratch_shapes=[pltpu.SemaphoreType.DMA((count,))],
+        compiler_params=pltpu.CompilerParams(vmem_limit_bytes=2 ** 20),
+    )(*arrays)
 
 
 def on_device(features, w_in, b_in, w_out, partner, window):
@@ -418,18 +442,19 @@
     loss, gwi, gbi, gwo = pl.pallas_call(
         functools.partial(kernel if keep else no_slope, n, rows, tile, a_chunk),
         out_shape=(
-            jax.ShapeDtypeStruct((1, A_DEV), F32),
-            jax.ShapeDtypeStruct((chan, half), F32),
-            jax.ShapeDtypeStruct((1, half), F32),
-            jax.ShapeDtypeStruct((half, embed), F32),
+            pltpu.VMEM((1, A_DEV), F32),
+            pltpu.VMEM((chan, half), F32),
+            pltpu.VMEM((1, half), F32),
+            pltpu.VMEM((half, embed), F32),
         ),
         in_specs=[vmem] * 5 + [pl.BlockSpec(memory_space=pltpu.SMEM)],
         out_specs=(vmem,) * 4,
         scratch_shapes=scratch,
         compiler_params=pltpu.CompilerParams(
-            collective_id=0, has_side_effects=True, vmem_limit_bytes=67043328
+            collective_id=0, has_side_effects=True, vmem_limit_bytes=64 * 2 ** 20 - 3 * 2 ** 20
         ),
     )(features, w_in, b_in.reshape(1, half), w_out, partner.reshape(1, rows), window)
+    loss, gwi, gbi, gwo = hand_out(loss, gwi, gbi, gwo)
     return (loss.reshape(A_DEV), gwi, gbi.reshape(half), gwo)
 
 

time: 45.6 us -> 41.4 us (0.908)
  local copies, waits for them, and re-layouts: 4.24 us -> 0 us
    unnamed x10 -> x0, local copies, waits for them, and re-layouts: 4.24 us -> none
    pallas_call x0 -> x1, Pallas kernels: none -> 0.87 us  [hand_out(): pl.pallas_call(copy_all, out_shape=[jax.ShapeDtypeStruct(a.shape, a.dtype...]
    pallas_call x1, Pallas kernels: 40.5 us -> 39.7 us  [on_device(): pl.pallas_call(functools.partial(kernel if keep else no_slope, n, rows, t...]
where the time goes in v4:
time: 41.4 us; the launch traced here: 41.2 us
  Pallas kernels  40.6 us (98%)
  between operations  0.64 us (2%)
    pallas_call x1, Pallas kernels, on_device(): pl.pallas_call(functools.partial(kernel if keep else no_slope, n, rows, t...  39.7 us
    pallas_call x1, Pallas kernels, hand_out(): pl.pallas_call(copy_all, out_shape=[jax.ShapeDtypeStruct(a.shape, a.dtype...  0.87 us

profile of v4, /device:TPU:0, one launch (start us, length us, event | category | flops | bytes accessed | tf_op | source)
XLA Modules:
  0.0 41.2 jit_solution(6632212895783781472)
XLA Ops:
  0.6 39.7 %shard_map.93 = (f32[1,32]{1,0:T(1,128)S(1)}, f32[512,256]{1,0:T(8,128)S(1)}, f32[1,256]{1,0:T(1,128)S(1)}, f32[256,128]{1,0:T(8,128)S(1)}) custom-call(bf16[128,512]{1,0:T(8,128)(2,1)} %f_ref.1, bf16[512,256]{1,0:T(8,128)(2,1)} %wi_ref.1, f32[1,256]{1,0:T(1,128)} %bitcast.4, bf16[256,128]{1,0:T(8,128)(2,1)} %wo_ref.1, s32[1,128]{1,0:T(1,128)} %bitcast.5, ...), custom_call_target="tpu_custom_call" | custom-call | tf_op jit(solution)/shard_map/pallas_call | solution.py:442
  40.4 0.9 %shard_map.94 = (f32[1,32]{1,0:T(1,128)}, f32[512,256]{1,0:T(8,128)}, f32[1,256]{1,0:T(1,128)}, f32[256,128]{1,0:T(8,128)}) custom-call(f32[1,32]{1,0:T(1,128)S(1)} %get-tuple-element.12.refs_0_, f32[512,256]{1,0:T(8,128)S(1)} %get-tuple-element.13.refs_1_, f32[1,256]{1,0:T(1,128)S(1)} %get-tuple-element.14.refs_2_, f32[256,128]{1,0:T(8,128)S(1)} %get-tuple-element.15.refs_3_), custom_call_target="tpu_custom_call" | custom-call | tf_op jit(solution)/shard_map/pallas_call | solution.py:396

commit v5 on v4

--- a/solution.py
+++ b/solution.py
@@ -257,7 +257,7 @@
         ids[at, :] = first + lax.broadcasted_iota(jnp.int32, (A_DEV, embed), 0)
         return 0
 
-    lax.fori_loop(0, n, gather, 0)
+    lax.fori_loop(0, n, gather, 0, unroll=4)
 
     blocks = tile // rows
     reps = tile // embed
@@ -274,7 +274,7 @@
         part[t] = v[0:1, :rows] * rows + v[0:1, rows:]
         return 0
 
-    lax.fori_loop(0, n, unpack, 0)
+    lax.fori_loop(0, n, unpack, 0, unroll=4)
 
     def part_row(t):
         pieces = [part[t * blocks + i] for i in range(blocks)]
@@ -297,11 +297,15 @@
         return (tot, hit + jnp.sum(h, axis=1, keepdims=True))
 
     zero = jnp.zeros((A_DEV, 1), F32)
-    tot, hit = lax.fori_loop(0, total // tile, own_tile, (zero, zero))
+    tot, hit = lax.fori_loop(
+        0, total // tile, own_tile, (zero, zero), unroll=total // tile <= 4
+    )
     loss = jnp.log(tot) + SHIFT - hit * INV_TEMP
     r_iota = lax.broadcasted_iota(jnp.int32, (A_DEV, A_DEV), 0)
     c_iota = lax.broadcasted_iota(jnp.int32, (A_DEV, A_DEV), 1)
     loss_ref[...] = jnp.sum(jnp.where(r_iota == c_iota, loss, 0.0), axis=0, keepdims=True)
+
+    few = total // tile <= 4
 
     def loss_chunk(k, _):
         base = pl.multiple_of(k * a_chunk, a_chunk)
@@ -318,7 +322,7 @@
             ex[:, pl.ds(start, tile)] = e
             return tot + jnp.sum(e, axis=1, keepdims=True)
 
-        tot = lax.fori_loop(0, total // tile, soft, jnp.zeros((a_chunk, 1), F32))
+        tot = lax.fori_loop(0, total // tile, soft, jnp.zeros((a_chunk, 1), F32), unroll=few)
         inv = 1.0 / tot
 
         def back(t, acc):
@@ -329,7 +333,9 @@
             gemb[at, :] += dot(w, anc, ((0,), (0,)))
             return acc + dot(w, emb[at, :])
 
-        row = lax.fori_loop(0, total // tile, back, jnp.zeros((a_chunk, embed), F32))
+        row = lax.fori_loop(
+            0, total // tile, back, jnp.zeros((a_chunk, embed), F32), unroll=few
+        )
         for i in range(a_chunk // A_DEV):
             b = k * (a_chunk // A_DEV) + i
             piece = row[i * A_DEV:(i + 1) * A_DEV, :]
@@ -366,7 +372,7 @@
         gbi_ref[...] += jnp.sum(gpre.astype(F32), axis=0, keepdims=True)
         return 0
 
-    lax.fori_loop(0, total // tile, grads, 0)
+    lax.fori_loop(0, total // tile, grads, 0, unroll=few)
 
     own_sends(False)
     first_step(False)

time: 41.4 us -> 37.1 us (0.90)
  Pallas kernels: 40.6 us -> 36.3 us
    pallas_call x1, Pallas kernels: 39.7 us -> 35.5 us  [on_device(): pl.pallas_call(functools.partial(kernel if keep else no_slope, n, rows, t...]
where the time goes in v5:
time: 37.1 us; the launch traced here: 37 us
  Pallas kernels  36.3 us (98%)
  between operations  0.64 us (2%)
    pallas_call x1, Pallas kernels, on_device(): pl.pallas_call(functools.partial(kernel if keep else no_slope, n, rows, t...  35.5 us
    pallas_call x1, Pallas kernels, hand_out(): pl.pallas_call(copy_all, out_shape=[jax.ShapeDtypeStruct(a.shape, a.dtype...  0.87 us

profile of v5, /device:TPU:0, one launch (start us, length us, event | category | flops | bytes accessed | tf_op | source)
XLA Modules:
  0.0 37.0 jit_solution(18416255262635210410)
XLA Ops:
  0.6 35.5 %shard_map.93 = (f32[1,32]{1,0:T(1,128)S(1)}, f32[512,256]{1,0:T(8,128)S(1)}, f32[1,256]{1,0:T(1,128)S(1)}, f32[256,128]{1,0:T(8,128)S(1)}) custom-call(bf16[128,512]{1,0:T(8,128)(2,1)} %f_ref.1, bf16[512,256]{1,0:T(8,128)(2,1)} %wi_ref.1, f32[1,256]{1,0:T(1,128)} %bitcast.4, bf16[256,128]{1,0:T(8,128)(2,1)} %wo_ref.1, s32[1,128]{1,0:T(1,128)} %bitcast.5, ...), custom_call_target="tpu_custom_call" | custom-call | tf_op jit(solution)/shard_map/pallas_call | solution.py:448
  36.1 0.9 %shard_map.94 = (f32[1,32]{1,0:T(1,128)}, f32[512,256]{1,0:T(8,128)}, f32[1,256]{1,0:T(1,128)}, f32[256,128]{1,0:T(8,128)}) custom-call(f32[1,32]{1,0:T(1,128)S(1)} %get-tuple-element.12.refs_0_, f32[512,256]{1,0:T(8,128)S(1)} %get-tuple-element.13.refs_1_, f32[1,256]{1,0:T(1,128)S(1)} %get-tuple-element.14.refs_2_, f32[256,128]{1,0:T(8,128)S(1)} %get-tuple-element.15.refs_3_), custom_call_target="tpu_custom_call" | custom-call | tf_op jit(solution)/shard_map/pallas_call | solution.py:402
